TPU v7x, 128 devices: a whole 4x4x4 slice. The times are simulated.
128 devices in a mesh: row: 8 (over z, y_lo), col: 16 (over x, y_hi, core).
Axes of the slice: x: 4, y: 4 (y_hi: 2, y_lo: 2; y = y_hi * 2 + y_lo), z: 4, core: 2. Of those that a mesh axis runs over, the one named last changes fastest.
Arguments:
- covariance: float32 [16384, 16384], P('row', 'col'), may hold values from -1 to 3, as said below
- center: float32 [16384], replicated, may hold values from 0.4 to 1
- links: float32 [4, 16384], replicated, may hold values from 0.05 to 0.25
- process: float32 [16384], replicated, may hold values from 0.1 to 1
- wells: int32 [1, 256], replicated, may hold values from 0 to 16383, as said below
- noise: float32 [1, 256], replicated, may hold values from 0.05 to 0.5
Outputs:
- updated: float32 [16384, 16384], P('row', 'col')
Inputs may be any that keep to these rules, and one draw needn't show every extreme that they name: `covariance`: symmetric positive definite. `wells`: each row holds 256 distinct cells; at most 32 of them lie in one aligned block of 1024 cells, and exactly 32 in some block.
All inputs are finite; a program needn't handle non-finite values.
Results may differ from a plain program's by a relative error of at most 0.0001.
Values sent between devices are 32-bit elements; how exact they have to be, the bound alone decides.
No kernel may reach another device: no remote copies, remote signals or barrier semaphores. Data moves between devices by JAX's collectives and lax.ppermute only.
A program may use at most 128 MiB of HBM per device.

v0:
```python
import jax
import jax.numpy as jnp
from jax import lax
from jax.sharding import PartitionSpec as P

NGY = 128
M = 256
WMAX = 32


def extended(cells, sides, width):
    for axis, dim in sides:
        count = lax.axis_size(axis)
        ends = count - 1
        head = lax.slice_in_dim(cells, 0, width, axis=dim)
        tail = lax.slice_in_dim(cells, cells.shape[dim] - width, cells.shape[dim], axis=dim)
        cells = jnp.concatenate(
            [
                lax.ppermute(tail, axis, [(i, (i + 1) % count) for i in range(ends)]),
                cells,
                lax.ppermute(head, axis, [((i + 1) % count, i) for i in range(ends)]),
            ],
            axis=dim,
        )
    return cells


def rows_first(arrays, axis, dims):
    turned = [jnp.moveaxis(a, dim, 0) for a, dim in zip(arrays, dims)]
    widths = [t[0].size for t in turned]
    both = jnp.concatenate([t.reshape(-1, w) for t, w in zip(turned, widths)], axis=1)
    result = lax.all_gather(both, axis, axis=0, tiled=True)
    blocks = jnp.split(result, [sum(widths[:k]) for k in range(1, len(widths))], axis=1)
    return tuple(
        (
            jnp.moveaxis(b.reshape(-1, *t.shape[1:]), 0, dim)
            for b, t, dim in zip(blocks, turned, dims)
        )
    )


def shards(covariance, center, links, process, wells, noise):
    row_id = lax.axis_index("row")
    col_id = lax.axis_index("col")
    row_count, col_count = covariance.shape
    grid_rows = row_count // NGY
    grid_cols = col_count // NGY
    row_start = row_id * row_count
    col_start = col_id * col_count
    own_rows = lax.dynamic_slice_in_dim(center, row_start, row_count).reshape(grid_rows, NGY, 1)
    link_rows = lax.dynamic_slice_in_dim(links, row_start, row_count, 1).reshape(
        4, grid_rows, NGY, 1
    )
    own_cols = lax.dynamic_slice_in_dim(center, col_start, col_count).reshape(1, grid_cols, NGY)
    link_cols = lax.dynamic_slice_in_dim(links, col_start, col_count, 1).reshape(
        4, 1, grid_cols, NGY
    )
    noise_rows = lax.dynamic_slice_in_dim(process, row_start, row_count)
    local_rows = jnp.arange(row_count, dtype=jnp.int32)
    diag_cols = row_start + local_rows - col_start
    diag_valid = (diag_cols >= 0) & (diag_cols < col_count)
    diag_clip = jnp.clip(diag_cols, 0, col_count - 1)
    diag_values = jnp.where(diag_valid, noise_rows, 0.0)
    current = covariance
    field = current.reshape(grid_rows, NGY, col_count)
    rimmed = extended(field, (("row", 0),), 1)
    padded = jnp.pad(rimmed, ((0, 0), (1, 1), (0, 0)))
    left = own_rows * field + link_rows[0] * padded[:-2, 1:-1] + link_rows[1] * padded[2:, 1:-1]
    left = left + link_rows[2] * padded[1:-1, :-2] + link_rows[3] * padded[1:-1, 2:]
    field = left.reshape(row_count, grid_cols, NGY)
    rimmed = extended(field, (("col", 1),), 1)
    padded = jnp.pad(rimmed, ((0, 0), (0, 0), (1, 1)))
    right = (
        own_cols * field + link_cols[0] * padded[:, :-2, 1:-1] + link_cols[1] * padded[:, 2:, 1:-1]
    )
    right = right + link_cols[2] * padded[:, 1:-1, :-2] + link_cols[3] * padded[:, 1:-1, 2:]
    predicted = right.reshape(row_count, col_count).at[local_rows, diag_clip].add(diag_values)
    chosen = wells[0]
    col_local = chosen - col_start
    in_col = (col_local >= 0) & (col_local < col_count)
    col_clip = jnp.clip(col_local, 0, col_count - 1)
    order = jnp.argsort(jnp.where(in_col, 0, 1).astype(jnp.int32), stable=True)[:WMAX]
    valid = in_col[order]
    compact = jnp.where(valid[None, :], jnp.take(predicted, col_clip[order], axis=1), 0.0)
    numbers = jnp.where(valid, order, -1).astype(jnp.float32)
    all_cols, all_numbers = rows_first((compact, numbers), "col", (1, 0))
    onehot = (all_numbers[:, None] == jnp.arange(M, dtype=jnp.float32)[None, :]).astype(jnp.float32)
    strip = jnp.dot(all_cols, onehot, precision=lax.Precision.HIGHEST)
    row_local = chosen - row_start
    in_row = (row_local >= 0) & (row_local < row_count)
    row_clip = jnp.clip(row_local, 0, row_count - 1)
    rows_part = jnp.where(in_row[:, None], jnp.take(predicted, row_clip, axis=0), 0.0)
    gram_part = jnp.where(in_row[:, None], jnp.take(strip, row_clip, axis=0), 0.0)
    across, gram = lax.psum((rows_part, gram_part), "row")
    innovation = gram + jnp.diag(noise[0])
    factor = jnp.linalg.cholesky(innovation)
    solved = jax.scipy.linalg.cho_solve((factor, True), across)
    current = predicted - jnp.dot(strip, solved, precision=lax.Precision.HIGHEST)
    return current


def solution(mesh):
    in_specs = (P("row", "col"), P(), P(), P(), P(), P())
    out_specs = P("row", "col")
    return jax.shard_map(shards, mesh=mesh, in_specs=in_specs, out_specs=out_specs, check_vma=False)
```

profile of v0, /device:TPU:0, one launch (start us, length us, event | category | flops | bytes accessed | tf_op | source)
XLA Modules:
  0.0 419.2 jit_solution(4098314979119295900)
XLA Ops:
  7.8 3.6 collective-permute-start
  14.9 3.2 sort.17
  22.6 13.5 %collective-permute-done.1 = f32[1,128,1024]{2,1,0:T(8,128)S(1)} collective-permute-done((f32[1,128,1024]{2,1,0:T(8,128)S(1)}, f32[1,128,1024]{2,1,0:T(8,128)S(1)}, u32[]{:S(2)}, u32[]{:S(2)}) %collective-permute-start.1) | collective-permute-done | bytes 524320 | tf_op jit(solution)/shard_map/ppermute | solution.py:21
  36.1 4.3 %select_maximum_fusion.2 = f32[18,130,1024]{2,1,0:T(8,128)S(1)} fusion(f32[1,128,1024]{2,1,0:T(8,128)S(1)} %collective-permute-done.1, f32[16,128,1024]{2,1,0:T(8,128)} %bitcast.73, f32[1,128,1024]{2,1,0:T(8,128)S(1)} %collective-permute-done), kind=kLoop, calls=%fused_computation.15 | loop fusion | flops 19169280 | bytes 19021824 | tf_op jit(solution)/shard_map/concatenate | solution.py:17
  40.3 9.5 %fusion.9 = f32[16,128,1024]{2,1,0:T(8,128)S(1)} fusion(f32[18,130,1024]{2,1,0:T(8,128)S(1)} %select_maximum_fusion.2, f32[1,128,1024]{2,1,0:T(8,128)S(1)} %collective-permute-done.1, f32[16,128,1024]{2,1,0:T(8,128)} %bitcast.74, f32[1,128,1024]{2,1,0:T(8,128)S(1)} %collective-permute-done, f32[16,128]{1,0:T(8,128)S(1)} %bitcast.79, ...), kind=kLoop, calls=%fused_computation.30 | loop fusion | flops 23068672 | bytes 34643968 | tf_op jit(solution)/shard_map/add | solution.py:69
  49.9 2.1 copy.32
  52.0 3.4 copy-done.2
  62.0 4.8 %collective-permute-done.3 = f32[2048,1,128]{2,1,0:T(1,128)S(1)} collective-permute-done((f32[2048,1,128]{2,1,0:T(1,128)S(1)}, f32[2048,1,128]{2,1,0:T(1,128)S(1)}, u32[]{:S(2)}, u32[]{:S(2)}) %collective-permute-start.3) | collective-permute-done | bytes 1048608 | tf_op jit(solution)/shard_map/ppermute | solution.py:21
  66.8 23.3 %select_maximum_fusion = f32[2048,10,130]{2,1,0:T(8,128)} fusion(f32[2048,1,128]{2,1,0:T(1,128)S(1)} %collective-permute-done.3, f32[2048,8,128]{2,1,0:T(8,128)} %bitcast.71, f32[2048,1,128]{2,1,0:T(1,128)S(1)} %collective-permute-done.2), kind=kLoop, calls=%fused_computation.10 | loop fusion | flops 21299200 | bytes 21135360 | tf_op jit(solution)/shard_map/concatenate | solution.py:17
  90.0 32.2 %fusion.3 = f32[2097152]{0:T(1024)} fusion(f32[2048,10,130]{2,1,0:T(8,128)} %select_maximum_fusion, f32[2048,1,128]{2,1,0:T(1,128)S(1)} %collective-permute-done.3, f32[2048,8,128]{2,1,0:T(8,128)} %bitcast.72, f32[2048,1,128]{2,1,0:T(1,128)S(1)} %collective-permute-done.2, f32[8,128]{1,0:T(8,128)S(1)} %bitcast.83, f32[8,128]{1,0:T(8,128)S(1)} %bitcast.81, ...), kind=kLoop, calls=%fused_computation.20 | loop fusion | flops 23068672 | bytes 35672064
  122.3 16.9 %scatter_fusion = f32[2097152]{0:T(1024)} fusion(f32[2097152]{0:T(1024)} %fusion.3, s32[2048]{0:T(1024)S(1)} %broadcast_select_fusion, f32[2048]{0:T(1024)S(1)} %dynamic-slice_select_fusion), kind=kCustom, calls=%fused_computation.5 | custom fusion | flops 2048 | bytes 32768
  139.1 9.2 %reshape.178 = f32[2048,1024]{1,0:T(8,128)} reshape(f32[2097152]{0:T(1024)} %scatter_fusion) | data formatting | bytes 16777216 | tf_op jit(solution)/shard_map/scatter-add | solution.py:77
  148.4 9.1 %copy.23 = f32[2048,1024]{0,1:T(8,128)} copy(f32[2048,1024]{1,0:T(8,128)} %reshape.178) | data formatting | bytes 16777216 | tf_op jit(solution)/shard_map/scatter-add | solution.py:77
  157.5 4.2 gather_fusion.2
  162.8 5.0 %gather_fusion.4 = f32[256,1024]{1,0:T(8,128)S(1)} fusion(f32[2048,1024]{1,0:T(8,128)} %reshape.178, s32[1024]{0:T(1024)S(1)} %pad_clamp_fusion), kind=kCustom, calls=%fused_computation.4 | custom fusion | bytes 2098176 | tf_op jit(solution)/shard_map/jit(_take)/gather | solution.py:92
  168.9 72.6 %all-gather.2.cloned.1.call-done = f32[512,2049]{1,0:T(8,128)} async-done(((f32[32,2049]{1,0:T(8,128)}), f32[512,2049]{1,0:T(8,128)}) %all-gather.2.cloned.1.call-update) | async-done | bytes 4196368 | tf_op jit(solution)/shard_map/all_gather | solution.py:32
  242.7 5.7 %fusion.15 = f32[2048,256]{1,0:T(8,128)S(1)} fusion(f32[512,2049]{1,0:T(8,128)} %all-gather.2.cloned.1.call-done, f32[512]{0:T(512)S(1)} %slice_reduce_fusion), kind=kOutput, calls=%fused_computation.40 | convolution fusion | flops 3221356544 | bytes 6293504 | tf_op jit(solution)/shard_map/dot_general | solution.py:88
  250.3 82.6 %all-reduce.6.cloned.1.call-done = (f32[256,1024]{1,0:T(8,128)}, f32[256,256]{0,1:T(8,128)}) async-done(((f32[256,1024]{1,0:T(8,128)}, f32[256,256]{0,1:T(8,128)}), (f32[256,1024]{1,0:T(8,128)}, f32[256,256]{0,1:T(8,128)})) %all-reduce.6.cloned.1.call-update) | async-done | bytes 1310736 | tf_op jit(solution)/shard_map/psum | solution.py:94
  334.9 11.7 %cholesky.48 = f32[128,128]{1,0:T(8,128)S(1)} custom-call(f32[128,128]{1,0:T(8,128)S(1)} %cholesky.112), custom_call_target="Cholesky" | custom-call | tf_op jit(solution)/shard_map/jit(cholesky)/cholesky | solution.py:96
  346.7 9.8 %custom-call.18 = f32[1,128,128]{1,2,0:T(8,128)S(1)} custom-call(f32[1,128,128]{2,1,0:T(8,128)S(1)} %get-tuple-element.56), custom_call_target="InvertDiagBlocksLowerTriangular" | custom-call | tf_op jit(solution)/shard_map/jit(cholesky)/cholesky | solution.py:96
  357.0 11.9 %cholesky.101 = f32[128,128]{1,0:T(8,128)S(1)} custom-call(f32[128,128]{1,0:T(8,128)S(1)} %convolution_subtract_fusion.3), custom_call_target="Cholesky" | custom-call | tf_op jit(solution)/shard_map/jit(cholesky)/cholesky | solution.py:96
  371.4 4.3 %while.1 = (s32[]{:T(128)}, f32[256,256]{0,1:T(8,128)S(1)}, s32[2,2]{1,0:T(2,128)S(1)}, f32[2,128,128]{2,1,0:T(8,128)S(1)}, s32[]{:T(128)}) while((s32[]{:T(128)}, f32[256,256]{0,1:T(8,128)S(1)}, s32[2,2]{1,0:T(2,128)S(1)}, f32[2,128,128]{2,1,0:T(8,128)S(1)}, s32[]{:T(128)}) %tuple.34), condition=%wide.while_cond, body=%wide.while_body.sunk | while | flops 2 | bytes 393321 | solution.py:97
  375.7 19.7 %custom-call.19 = f32[2,128,128]{1,2,0:T(8,128)S(1)} custom-call(f32[2,128,128]{2,1,0:T(8,128)S(1)} %get-tuple-element.14), custom_call_target="InvertDiagBlocksLowerTriangular" | custom-call | tf_op jit(solution)/shard_map/jit(_cho_solve)/triangular_solve | solution.py:97
  401.1 11.0 %convolution_subtract_fusion = f32[2048,1024]{1,0:T(8,128)} fusion(f32[2048,1024]{1,0:T(8,128)} %reshape.178, f32[2048,256]{1,0:T(8,128)S(1)} %fusion.15, f32[128,1024]{1,0:T(8,128)S(1)} %fusion.28, f32[128,1024]{1,0:T(8,128)S(1)} %fusion.27), kind=kOutput, calls=%fused_computation.39 | convolution fusion | flops 6444810240 | bytes 19922944 | tf_op jit(solution)/shard_map/dot_general | solution.py:98
  (92 shorter events, 34.6 us)
Async XLA Ops:
  6.5 7.6 %copy-start = (f32[16384]{0:T(1024)S(1)}, f32[16384]{0:T(1024)}, u32[]{:S(2)}) copy-start(f32[16384]{0:T(1024)} %param.7) | copy-start | bytes 196612
  6.5 235.0 %all-gather.2.cloned.1.call-start = ((), (), s32[]{:S(2)}) async-start(), calls=%async_computation | async-start | bytes 4734976 | tf_op jit(solution)/shard_map/all_gather | solution.py:32
  7.8 14.7 %collective-permute-start = (f32[1,128,1024]{2,1,0:T(8,128)S(1)}, f32[1,128,1024]{2,1,0:T(8,128)S(1)}, u32[]{:S(2)}, u32[]{:S(2)}) collective-permute-start(f32[1,128,1024]{2,1,0:T(8,128)S(1)} %get-tuple-element.45), channel_id=1, source_target_pairs={{0,16},{16,32},{32,48},{48,64},{64,80},{80,96},{96,112},{1,17},{17... | collective-permute-start | bytes 1572872 | tf_op jit(solution)/shard_map/ppermute | solution.py:19
  11.4 24.6 %collective-permute-start.1 = (f32[1,128,1024]{2,1,0:T(8,128)S(1)}, f32[1,128,1024]{2,1,0:T(8,128)S(1)}, u32[]{:S(2)}, u32[]{:S(2)}) collective-permute-start(f32[1,128,1024]{2,1,0:T(8,128)S(1)} %get-tuple-element.46), channel_id=1, source_target_pairs={{16,0},{32,16},{48,32},{64,48},{80,64},{96,80},{112,96},{17,1},{33... | collective-permute-start | bytes 1572872 | tf_op jit(solution)/shard_map/ppermute | solution.py:21
  49.9 11.8 %copy-start.6 = (s32[2]{0:T(128)S(1)}, s32[2]{0:T(128)}, u32[]{:S(2)}) copy-start(s32[2]{0:T(128)} %constant.169) | copy-start | bytes 28
  49.9 11.9 %copy-start.5 = (s32[2]{0:T(128)S(1)}, s32[2]{0:T(128)}, u32[]{:S(2)}) copy-start(s32[2]{0:T(128)} %constant.172) | copy-start | bytes 28
  52.0 3.4 copy-start.2
  57.5 4.5 %collective-permute-start.2 = (f32[2048,1,128]{2,1,0:T(1,128)}, f32[2048,1,128]{2,1,0:T(1,128)S(1)}, u32[]{:S(2)}, u32[]{:S(2)}) collective-permute-start(f32[2048,1,128]{2,1,0:T(1,128)} %get-tuple-element.43), channel_id=1, source_target_pairs={{0,1},{1,2},{2,3},{3,4},{4,5},{5,6},{6,7},{7,8},{8,9},{9,10},{10,1... | collective-permute-start | bytes 3145736 | tf_op jit(solution)/shard_map/ppermute | solution.py:19
  58.8 7.9 %collective-permute-start.3 = (f32[2048,1,128]{2,1,0:T(1,128)S(1)}, f32[2048,1,128]{2,1,0:T(1,128)S(1)}, u32[]{:S(2)}, u32[]{:S(2)}) collective-permute-start(f32[2048,1,128]{2,1,0:T(1,128)S(1)} %get-tuple-element.44), channel_id=1, source_target_pairs={{1,0},{2,1},{3,2},{4,3},{5,4},{6,5},{7,6},{8,7},{9,8},{10,9},{11,1... | collective-permute-start | bytes 3145736 | tf_op jit(solution)/shard_map/ppermute | solution.py:21
  157.5 5.3 %copy-start.3 = (s32[1,256]{1,0:T(1,128)S(1)}, s32[1,256]{1,0:T(1,128)}, u32[]{:S(2)}) copy-start(s32[1,256]{1,0:T(1,128)} %param.10) | copy-start | bytes 3076
  162.5 170.3 %all-reduce.6.cloned.1.call-start = ((), (), s32[]{:S(2)}) async-start(), calls=%async_computation.1 | async-start | bytes 2621440 | tf_op jit(solution)/shard_map/psum | solution.py:94
  167.8 165.1 %copy-start.4 = (f32[1,256]{1,0:T(1,128)S(1)}, f32[1,256]{1,0:T(1,128)}, u32[]{:S(2)}) copy-start(f32[1,256]{1,0:T(1,128)} %param.11) | copy-start | bytes 3076
  400.5 11.6 %copy-start.1 = (f32[16384]{0:T(1024)S(1)}, f32[16384]{0:T(1024)}, u32[]{:S(2)}) copy-start(f32[16384]{0:T(1024)} %param.7) | copy-start | bytes 196612
Sparse Core Ops, SparseCore 0:
  162.7 78.8 all-gather.1
  250.4 82.4 all-reduce.5
where the time goes:
time: 425 us; the launch traced here: 419 us
  waiting for transfers between devices  176 us (41%)
  other arithmetic  150 us (35%)
  local copies, waits for them, and re-layouts  46.8 us (11%)
  matrix products  22.9 us (5%)
  between operations  15.3 us (4%)
  starting transfers between devices  8.21 us (2%)
    psum x1, waiting for transfers between devices, shards(): across, gram = lax.psum((rows_part, gram_part), 'row')  82.6 us
    all_gather x1, waiting for transfers between devices, rows_first(): result = lax.all_gather(both, axis, axis=0, tiled=True)  72.6 us
    unnamed x6, other arithmetic  49.3 us
    another operation x6, other arithmetic, shards(): factor = jnp.linalg.cholesky(innovation)  34.2 us
    concatenate x2, other arithmetic, extended(): jnp.concatenate([lax.ppermute(tail, axis, [(i, (i + 1) % count) for i in...  27.6 us
    another operation x3, other arithmetic, shards(): solved = jax.scipy.linalg.cho_solve((factor, True), across)  19.7 us
    scatter-add x2, local copies, waits for them, and re-layouts, shards(): right.reshape(row_count, col_count).at[local_rows, diag_clip]  18.4 us
    ppermute x2, waiting for transfers between devices, extended(): lax.ppermute(head, axis, [((i + 1) % count, i) for i in range(ends)])  18.3 us
  transfers between devices with their start and end apart: 6, of which 5 were waited for; matrix products, arithmetic and copies ran while one was open for 4% of the time, Pallas kernels for 0%

commit v1 on v0

--- a/solution.py
+++ b/solution.py
@@ -29,7 +29,9 @@
     turned = [jnp.moveaxis(a, dim, 0) for a, dim in zip(arrays, dims)]
     widths = [t[0].size for t in turned]
     both = jnp.concatenate([t.reshape(-1, w) for t, w in zip(turned, widths)], axis=1)
-    result = lax.all_gather(both, axis, axis=0, tiled=True)
+    result = jnp.concatenate(
+        lax.all_to_all(jnp.stack([both] * lax.axis_size(axis)), axis, 0, 0), axis=0
+    )
     blocks = jnp.split(result, [sum(widths[:k]) for k in range(1, len(widths))], axis=1)
     return tuple(
         (

time: 425 us -> 441 us (1.038)
  starting transfers between devices: 8.21 us -> 35.1 us
  waiting for transfers between devices: 176 us -> 162 us
    all_gather x1 -> x0, waiting for transfers between devices: 72.6 us -> none  [rows_first(): result = lax.all_gather(both, axis, axis=0, tiled=True)]
    all_to_all x0 -> x1, waiting for transfers between devices: none -> 50 us  [rows_first(): lax.all_to_all(jnp.stack([both] * lax.axis_size(axis)), axis, 0, 0)]
    all_to_all x0 -> x1, starting transfers between devices: none -> 26.9 us  [rows_first(): lax.all_to_all(jnp.stack([both] * lax.axis_size(axis)), axis, 0, 0)]
    psum x1, waiting for transfers between devices: 82.6 us -> 91.9 us  [shards(): across, gram = lax.psum((rows_part, gram_part), 'row')]
where the time goes in v1:
time: 441 us; the launch traced here: 435 us
  waiting for transfers between devices  162 us (37%)
  other arithmetic  150 us (34%)
  local copies, waits for them, and re-layouts  49.3 us (11%)
  starting transfers between devices  35.1 us (8%)
  matrix products  22.9 us (5%)
  between operations  15.4 us (3%)
    psum x1, waiting for transfers between devices, shards(): across, gram = lax.psum((rows_part, gram_part), 'row')  91.9 us
    all_to_all x1, waiting for transfers between devices, rows_first(): lax.all_to_all(jnp.stack([both] * lax.axis_size(axis)), axis, 0, 0)  50 us
    unnamed x6, other arithmetic  49.3 us
    another operation x6, other arithmetic, shards(): factor = jnp.linalg.cholesky(innovation)  34.2 us
    concatenate x2, other arithmetic, extended(): jnp.concatenate([lax.ppermute(tail, axis, [(i, (i + 1) % count) for i in...  27.6 us
    all_to_all x1, starting transfers between devices, rows_first(): lax.all_to_all(jnp.stack([both] * lax.axis_size(axis)), axis, 0, 0)  26.9 us
    another operation x3, other arithmetic, shards(): solved = jax.scipy.linalg.cho_solve((factor, True), across)  19.7 us
    scatter-add x2, local copies, waits for them, and re-layouts, shards(): right.reshape(row_count, col_count).at[local_rows, diag_clip]  18.4 us
  transfers between devices with their start and end apart: 6, of which 5 were waited for; matrix products, arithmetic and copies ran while one was open for 4% of the time, Pallas kernels for 0%

profile of v1, /device:TPU:0, one launch (start us, length us, event | category | flops | bytes accessed | tf_op | source)
XLA Modules:
  0.0 434.6 jit_solution(6711457977138542496)
XLA Ops:
  7.8 3.6 collective-permute-start
  14.9 3.2 sort.17
  22.6 13.5 %collective-permute-done.1 = f32[1,128,1024]{2,1,0:T(8,128)S(1)} collective-permute-done((f32[1,128,1024]{2,1,0:T(8,128)S(1)}, f32[1,128,1024]{2,1,0:T(8,128)S(1)}, u32[]{:S(2)}, u32[]{:S(2)}) %collective-permute-start.1) | collective-permute-done | bytes 524320 | tf_op jit(solution)/shard_map/ppermute | solution.py:21
  36.1 4.3 select_maximum_fusion.2
  40.3 9.5 %fusion.9 = f32[16,128,1024]{2,1,0:T(8,128)S(1)} fusion(f32[18,130,1024]{2,1,0:T(8,128)S(1)} %select_maximum_fusion.2, f32[1,128,1024]{2,1,0:T(8,128)S(1)} %collective-permute-done.1, f32[16,128,1024]{2,1,0:T(8,128)} %bitcast.75, f32[1,128,1024]{2,1,0:T(8,128)S(1)} %collective-permute-done, f32[16,128]{1,0:T(8,128)S(1)} %bitcast.80, ...), kind=kLoop, calls=%fused_computation.30 | loop fusion | flops 23068672 | bytes 34643968 | tf_op jit(solution)/shard_map/add | solution.py:71
  52.0 3.4 copy-done.2
  62.0 4.8 %collective-permute-done.3 = f32[2048,1,128]{2,1,0:T(1,128)S(1)} collective-permute-done((f32[2048,1,128]{2,1,0:T(1,128)S(1)}, f32[2048,1,128]{2,1,0:T(1,128)S(1)}, u32[]{:S(2)}, u32[]{:S(2)}) %collective-permute-start.3) | collective-permute-done | bytes 1048608 | tf_op jit(solution)/shard_map/ppermute | solution.py:21
  66.8 23.3 %select_maximum_fusion = f32[2048,10,130]{2,1,0:T(8,128)} fusion(f32[2048,1,128]{2,1,0:T(1,128)S(1)} %collective-permute-done.3, f32[2048,8,128]{2,1,0:T(8,128)} %bitcast.72, f32[2048,1,128]{2,1,0:T(1,128)S(1)} %collective-permute-done.2), kind=kLoop, calls=%fused_computation.10 | loop fusion | flops 21299200 | bytes 21135360 | tf_op jit(solution)/shard_map/concatenate | solution.py:17
  90.0 32.2 %fusion.3 = f32[2097152]{0:T(1024)} fusion(f32[2048,10,130]{2,1,0:T(8,128)} %select_maximum_fusion, f32[2048,1,128]{2,1,0:T(1,128)S(1)} %collective-permute-done.3, f32[2048,8,128]{2,1,0:T(8,128)} %bitcast.73, f32[2048,1,128]{2,1,0:T(1,128)S(1)} %collective-permute-done.2, f32[8,128]{1,0:T(8,128)S(1)} %bitcast.84, f32[8,128]{1,0:T(8,128)S(1)} %bitcast.82, ...), kind=kLoop, calls=%fused_computation.20 | loop fusion | flops 23068672 | bytes 35672064
  122.3 16.9 %scatter_fusion = f32[2097152]{0:T(1024)} fusion(f32[2097152]{0:T(1024)} %fusion.3, s32[2048]{0:T(1024)S(1)} %broadcast_select_fusion, f32[2048]{0:T(1024)S(1)} %dynamic-slice_select_fusion), kind=kCustom, calls=%fused_computation.5 | custom fusion | flops 2048 | bytes 32768
  139.1 9.2 %reshape.184 = f32[2048,1024]{1,0:T(8,128)} reshape(f32[2097152]{0:T(1024)} %scatter_fusion) | data formatting | bytes 16777216 | tf_op jit(solution)/shard_map/scatter-add | solution.py:79
  148.4 9.1 %copy.32 = f32[2048,1024]{0,1:T(8,128)} copy(f32[2048,1024]{1,0:T(8,128)} %reshape.184) | data formatting | bytes 16777216 | tf_op jit(solution)/shard_map/scatter-add | solution.py:79
  157.5 4.1 gather_fusion.2
  164.3 26.9 %all-to-all-start = ((f32[16,32,2049]{2,1,0:T(8,128)}), f32[16,32,2049]{2,1,0:T(8,128)}, u32[]{:S(2)}, u32[]{:S(2)}) async-start(f32[16,32,2049]{2,1,0:T(8,128)} %stack.2), calls=%async_computation | async-start | bytes 8912896 | tf_op jit(solution)/shard_map/all_to_all | solution.py:33
  191.5 5.0 %gather_fusion.4 = f32[256,1024]{1,0:T(8,128)S(1)} fusion(f32[2048,1024]{1,0:T(8,128)} %reshape.184, s32[1024]{0:T(1024)S(1)} %pad_clamp_fusion), kind=kCustom, calls=%fused_computation.4 | custom fusion | bytes 2098176 | tf_op jit(solution)/shard_map/jit(_take)/gather | solution.py:94
  197.7 50.0 %all-to-all-done = f32[16,32,2049]{2,1,0:T(8,128)} async-done(((f32[16,32,2049]{2,1,0:T(8,128)}), f32[16,32,2049]{2,1,0:T(8,128)}, u32[]{:S(2)}, u32[]{:S(2)}) %all-to-all-start) | async-done | bytes 4196384 | tf_op jit(solution)/shard_map/all_to_all | solution.py:33
  248.8 5.7 %fusion.15 = f32[2048,256]{1,0:T(8,128)S(1)} fusion(f32[512,2049]{1,0:T(8,128)} %bitcast.18, f32[512]{0:T(512)S(1)} %slice_reduce_fusion), kind=kOutput, calls=%fused_computation.40 | convolution fusion | flops 3221356544 | bytes 6293504 | tf_op jit(solution)/shard_map/dot_general | solution.py:90
  256.4 91.9 %all-reduce.6.cloned.1.call-done = (f32[256,1024]{1,0:T(8,128)}, f32[256,256]{0,1:T(8,128)}) async-done(((f32[256,1024]{1,0:T(8,128)}, f32[256,256]{0,1:T(8,128)}), (f32[256,1024]{1,0:T(8,128)}, f32[256,256]{0,1:T(8,128)})) %all-reduce.6.cloned.1.call-update) | async-done | bytes 1310736 | tf_op jit(solution)/shard_map/psum | solution.py:96
  350.4 11.7 %cholesky.48 = f32[128,128]{1,0:T(8,128)S(1)} custom-call(f32[128,128]{1,0:T(8,128)S(1)} %cholesky.112), custom_call_target="Cholesky" | custom-call | tf_op jit(solution)/shard_map/jit(cholesky)/cholesky | solution.py:98
  362.1 9.8 %custom-call.18 = f32[1,128,128]{1,2,0:T(8,128)S(1)} custom-call(f32[1,128,128]{2,1,0:T(8,128)S(1)} %get-tuple-element.60), custom_call_target="InvertDiagBlocksLowerTriangular" | custom-call | tf_op jit(solution)/shard_map/jit(cholesky)/cholesky | solution.py:98
  372.4 11.9 %cholesky.101 = f32[128,128]{1,0:T(8,128)S(1)} custom-call(f32[128,128]{1,0:T(8,128)S(1)} %convolution_subtract_fusion.3), custom_call_target="Cholesky" | custom-call | tf_op jit(solution)/shard_map/jit(cholesky)/cholesky | solution.py:98
  386.8 4.3 while.1
  391.1 19.7 %custom-call.19 = f32[2,128,128]{1,2,0:T(8,128)S(1)} custom-call(f32[2,128,128]{2,1,0:T(8,128)S(1)} %get-tuple-element.14), custom_call_target="InvertDiagBlocksLowerTriangular" | custom-call | tf_op jit(solution)/shard_map/jit(_cho_solve)/triangular_solve | solution.py:99
  416.6 11.0 %convolution_subtract_fusion = f32[2048,1024]{1,0:T(8,128)} fusion(f32[2048,1024]{1,0:T(8,128)} %reshape.184, f32[2048,256]{1,0:T(8,128)S(1)} %fusion.15, f32[128,1024]{1,0:T(8,128)S(1)} %fusion.28, f32[128,1024]{1,0:T(8,128)S(1)} %fusion.27), kind=kOutput, calls=%fused_computation.39 | convolution fusion | flops 6444810240 | bytes 19922944 | tf_op jit(solution)/shard_map/dot_general | solution.py:100
  (92 shorter events, 38.6 us)
Async XLA Ops:
  6.5 7.6 %copy-start = (f32[16384]{0:T(1024)S(1)}, f32[16384]{0:T(1024)}, u32[]{:S(2)}) copy-start(f32[16384]{0:T(1024)} %param.7) | copy-start | bytes 196612
  7.8 14.7 %collective-permute-start = (f32[1,128,1024]{2,1,0:T(8,128)S(1)}, f32[1,128,1024]{2,1,0:T(8,128)S(1)}, u32[]{:S(2)}, u32[]{:S(2)}) collective-permute-start(f32[1,128,1024]{2,1,0:T(8,128)S(1)} %get-tuple-element.49), channel_id=1, source_target_pairs={{0,16},{16,32},{32,48},{48,64},{64,80},{80,96},{96,112},{1,17},{17... | collective-permute-start | bytes 1572872 | tf_op jit(solution)/shard_map/ppermute | solution.py:19
  11.4 24.6 %collective-permute-start.1 = (f32[1,128,1024]{2,1,0:T(8,128)S(1)}, f32[1,128,1024]{2,1,0:T(8,128)S(1)}, u32[]{:S(2)}, u32[]{:S(2)}) collective-permute-start(f32[1,128,1024]{2,1,0:T(8,128)S(1)} %get-tuple-element.50), channel_id=1, source_target_pairs={{16,0},{32,16},{48,32},{64,48},{80,64},{96,80},{112,96},{17,1},{33... | collective-permute-start | bytes 1572872 | tf_op jit(solution)/shard_map/ppermute | solution.py:21
  49.9 11.8 %copy-start.6 = (s32[2]{0:T(128)S(1)}, s32[2]{0:T(128)}, u32[]{:S(2)}) copy-start(s32[2]{0:T(128)} %constant.169) | copy-start | bytes 28
  49.9 11.9 %copy-start.5 = (s32[2]{0:T(128)S(1)}, s32[2]{0:T(128)}, u32[]{:S(2)}) copy-start(s32[2]{0:T(128)} %constant.172) | copy-start | bytes 28
  52.0 3.4 copy-start.2
  57.5 4.5 %collective-permute-start.2 = (f32[2048,1,128]{2,1,0:T(1,128)}, f32[2048,1,128]{2,1,0:T(1,128)S(1)}, u32[]{:S(2)}, u32[]{:S(2)}) collective-permute-start(f32[2048,1,128]{2,1,0:T(1,128)} %get-tuple-element.47), channel_id=1, source_target_pairs={{0,1},{1,2},{2,3},{3,4},{4,5},{5,6},{6,7},{7,8},{8,9},{9,10},{10,1... | collective-permute-start | bytes 3145736 | tf_op jit(solution)/shard_map/ppermute | solution.py:19
  58.8 7.9 %collective-permute-start.3 = (f32[2048,1,128]{2,1,0:T(1,128)S(1)}, f32[2048,1,128]{2,1,0:T(1,128)S(1)}, u32[]{:S(2)}, u32[]{:S(2)}) collective-permute-start(f32[2048,1,128]{2,1,0:T(1,128)S(1)} %get-tuple-element.48), channel_id=1, source_target_pairs={{1,0},{2,1},{3,2},{4,3},{5,4},{6,5},{7,6},{8,7},{9,8},{10,9},{11,1... | collective-permute-start | bytes 3145736 | tf_op jit(solution)/shard_map/ppermute | solution.py:21
  161.6 29.8 %copy-start.3 = (s32[1,256]{1,0:T(1,128)S(1)}, s32[1,256]{1,0:T(1,128)}, u32[]{:S(2)}) copy-start(s32[1,256]{1,0:T(1,128)} %param.10) | copy-start | bytes 3076
  164.3 83.4 %all-to-all-start = ((f32[16,32,2049]{2,1,0:T(8,128)}), f32[16,32,2049]{2,1,0:T(8,128)}, u32[]{:S(2)}, u32[]{:S(2)}) async-start(f32[16,32,2049]{2,1,0:T(8,128)} %stack.2), calls=%async_computation | async-start | bytes 8912896 | tf_op jit(solution)/shard_map/all_to_all | solution.py:33
  191.2 157.1 %all-reduce.6.cloned.1.call-start = ((), (), s32[]{:S(2)}) async-start(), calls=%async_computation.1 | async-start | bytes 2621440 | tf_op jit(solution)/shard_map/psum | solution.py:96
  196.4 151.8 %copy-start.4 = (f32[1,256]{1,0:T(1,128)S(1)}, f32[1,256]{1,0:T(1,128)}, u32[]{:S(2)}) copy-start(f32[1,256]{1,0:T(1,128)} %param.11) | copy-start | bytes 3076
  416.0 11.6 %copy-start.1 = (f32[16384]{0:T(1024)S(1)}, f32[16384]{0:T(1024)}, u32[]{:S(2)}) copy-start(f32[16384]{0:T(1024)} %param.7) | copy-start | bytes 196612
Sparse Core Ops, SparseCore 0:
  256.5 91.7 all-reduce.5
